TPU v7x, 512 devices: a whole 4x4x16 slice. The times are simulated.
512 devices in a mesh: seq: 32 (over z, core), hid: 16 (over x, y).
Axes of the slice: x: 4, y: 4, z: 16, core: 2. Of those that a mesh axis runs over, the one named last changes fastest.
Arguments:
- activations: bfloat16 [16384, 4096], P('seq'), may hold values from -6 to 6
- w_inner: bfloat16 [4096, 4096], P('seq', 'hid'), may hold values from -0.09375 to 0.09375
- w_gate: bfloat16 [4096, 4096], P('seq', 'hid'), may hold values from -0.09375 to 0.09375
- w_groups: bfloat16 [4096, 1024], P('seq'), may hold values from -0.09375 to 0.09375
- w_step: bfloat16 [4096, 64], P('seq'), may hold values from -0.09375 to 0.09375
- w_out: bfloat16 [4096, 4096], P('seq', 'hid'), may hold values from -0.09375 to 0.09375
- conv_inner: float32 [4, 4096], P(None, 'hid'), may hold values from -3 to 3
- conv_groups: float32 [4, 1024], replicated, may hold values from -3 to 3
- step_bias: float32 [64], P('hid'), may hold values from -4 to 0
- decay_log: float32 [64], P('hid'), may hold values from -9 to -1
- skip_gain: float32 [64], P('hid'), may hold values from 0.5 to 1.5
- norm_gain: float32 [4096], P('hid'), may hold values from 0.5 to 1.5
Outputs:
- layer_out: bfloat16 [16384, 4096], P('seq', 'hid')
All inputs are finite; a program needn't handle non-finite values.
Results may differ from a plain program's by a relative error of at most 0.02.
Values may be sent and summed in bfloat16 or wider, within the bound.
A program may use at most 64 MiB of HBM per device.

v0:
```python
import jax
import jax.numpy as jnp
from jax import lax
from jax.sharding import PartitionSpec as P

HEADS = 64
P_SIZE = 64
N = 128
G = 4
Q = 256
K = 4
INNER = 4096


def from_behind(block, axis, distance):
    devices = range(lax.axis_size(axis))
    route = [(i - distance, i) for i in devices if i - distance in devices]
    return lax.ppermute(block, axis, route)


def carried_in(array, axis, join, neutral):
    place = lax.axis_index(axis)
    gathered = jax.tree.map(
        lambda a, kind: lax.all_gather(a.astype(kind), axis), array, (jnp.bfloat16, jnp.bfloat16)
    )
    state = jax.tree.map(lambda a, e: jnp.zeros_like(a) + jnp.asarray(e, a.dtype), array, neutral)

    def one(step, state):
        return join(
            state,
            jax.tree.map(
                lambda a, own: lax.dynamic_index_in_dim(a, step, 0, False).astype(own.dtype),
                gathered,
                array,
            ),
        )

    return lax.fori_loop(0, place, one, state)


def causal_conv(values, before, kernel):
    length = values.shape[0]
    extended = jnp.concatenate([before, values], axis=0)
    summed = jnp.zeros(values.shape, jnp.float32)
    for position in range(kernel.shape[0]):
        summed = (
            summed + extended[position : position + length].astype(jnp.float32) * kernel[position]
        )
    return jax.nn.silu(summed).astype(jnp.bfloat16)


def combine_states(earlier, later):
    return (earlier[0] * later[0], later[0][:, None, None] * earlier[1] + later[1])


def roll_state(state, inputs):
    total_here, fresh_here = inputs
    return (jnp.exp(total_here)[:, None, None] * state + fresh_here, state)


def local(
    activations,
    w_inner,
    w_gate,
    w_groups,
    w_step,
    w_out,
    conv_inner,
    conv_groups,
    step_bias,
    decay_log,
    skip_gain,
    norm_gain,
):
    tok_rows = activations.shape[0]
    heads_dev = step_bias.shape[0]
    width_dev = w_inner.shape[1]
    head_block = lax.axis_index("hid")
    group_cols = 2 * N
    group_index = head_block * heads_dev // (HEADS // G)
    step_cols = lax.dynamic_slice_in_dim(w_step, head_block * heads_dev, heads_dev, 1)
    own_cols = lax.dynamic_slice_in_dim(w_groups, group_index * group_cols, group_cols, 1)
    piece_inner = lax.all_gather(w_inner, "seq", axis=0, tiled=True)
    piece_gate = lax.all_gather(w_gate, "seq", axis=0, tiled=True)
    piece_groups = lax.all_gather(own_cols, "seq", axis=0, tiled=True)
    piece_step = lax.all_gather(step_cols, "seq", axis=0, tiled=True)
    piece_out = lax.all_gather(w_out, "seq", axis=0, tiled=True)
    acc_inner = jnp.dot(activations, piece_inner, preferred_element_type=jnp.float32)
    acc_gate = jnp.dot(activations, piece_gate, preferred_element_type=jnp.float32)
    acc_groups = jnp.dot(activations, piece_groups, preferred_element_type=jnp.float32)
    acc_step = jnp.dot(activations, piece_step, preferred_element_type=jnp.float32)
    groups_in = acc_groups.astype(jnp.bfloat16)
    inner_in = acc_inner.astype(jnp.bfloat16)
    gate_in = acc_gate.astype(jnp.bfloat16)
    conv_group = lax.dynamic_slice_in_dim(conv_groups, group_index * group_cols, group_cols, 1)
    tail_rows = K - 1
    inner_prev, groups_prev = from_behind(
        (inner_in[tok_rows - tail_rows :], groups_in[tok_rows - tail_rows :]), "seq", 1
    )
    inner_conv = causal_conv(inner_in, inner_prev, conv_inner)
    groups_conv = causal_conv(groups_in, groups_prev, conv_group)
    step_size = jax.nn.softplus(acc_step + step_bias)
    rates = -jnp.exp(decay_log)
    span_count = tok_rows // Q
    heads_x = inner_conv.reshape(span_count, Q, heads_dev, P_SIZE)
    b_in = groups_conv[:, :N].reshape(span_count, Q, N)
    c_out = groups_conv[:, N:].reshape(span_count, Q, N)
    block_dt = step_size.reshape(span_count, Q, heads_dev)
    cum_decay = jnp.cumsum(block_dt * rates, axis=1)
    scores = jnp.einsum("ctn,csn->cts", c_out, b_in, preferred_element_type=jnp.float32)
    ahead = jnp.arange(Q)[:, None] >= jnp.arange(Q)[None, :]
    decay_t = jnp.swapaxes(cum_decay, 1, 2)
    gap = jnp.where(ahead, decay_t[:, :, :, None] - decay_t[:, :, None, :], -1e30)
    mixing = (scores[:, None] * jnp.exp(gap) * jnp.swapaxes(block_dt, 1, 2)[:, :, None, :]).astype(
        jnp.bfloat16
    )
    intra = jnp.einsum("chts,cshp->cthp", mixing, heads_x, preferred_element_type=jnp.float32)
    span_total = cum_decay[:, -1]
    weights_in = jnp.exp(span_total[:, None, :] - cum_decay) * block_dt
    weighted = (b_in[:, :, None, :] * weights_in[:, :, :, None]).astype(jnp.bfloat16)
    fresh = jnp.einsum("cshn,cshp->chnp", weighted, heads_x, preferred_element_type=jnp.float32)
    zero_state = jnp.zeros((heads_dev, N, P_SIZE), jnp.float32)
    local_end, starts = lax.scan(roll_state, zero_state, (span_total, fresh))
    log_total = jnp.sum(span_total, axis=0)
    prior = jnp.cumsum(span_total, axis=0) - span_total
    identity = (jnp.ones((heads_dev,), jnp.float32), zero_state)
    state_in = carried_in((jnp.exp(log_total), local_end), "seq", combine_states, identity)[1]
    span_in = starts + jnp.exp(prior)[:, :, None, None] * state_in[None]
    inter = jnp.einsum(
        "ctn,chnp->cthp", c_out.astype(jnp.float32), span_in, precision=lax.Precision.HIGHEST
    )
    inter = inter * jnp.exp(cum_decay)[:, :, :, None]
    mixed = (intra + inter).reshape(tok_rows, width_dev) + jnp.repeat(
        skip_gain, P_SIZE
    ) * inner_conv.astype(jnp.float32)
    gated = mixed * jax.nn.silu(gate_in.astype(jnp.float32))
    squares = lax.psum(jnp.sum(gated * gated, axis=1), "hid")
    normed = (gated * lax.rsqrt(squares / INNER + 1e-05)[:, None] * norm_gain).astype(jnp.bfloat16)
    terms = lax.dot_general(
        normed, piece_out, (((1,), (1,)), ((), ())), preferred_element_type=jnp.float32
    )
    return lax.psum_scatter(terms.astype(jnp.bfloat16), "hid", scatter_dimension=1, tiled=True)


def solution(mesh):
    in_specs = (
        P("seq", None),
        P("seq", "hid"),
        P("seq", "hid"),
        P("seq", None),
        P("seq", None),
        P("seq", "hid"),
        P(None, "hid"),
        P(),
        P("hid"),
        P("hid"),
        P("hid"),
        P("hid"),
    )
    out_specs = P("seq", "hid")
    return jax.shard_map(local, mesh=mesh, in_specs=in_specs, out_specs=out_specs, check_vma=False)
```

profile of v0, /device:TPU:32, one launch (start us, length us, event | category | flops | bytes accessed | tf_op | source)
XLA Modules:
  0.0 480.8 jit_solution(4946631433308588536)
XLA Ops:
  6.5 0.9 copy-done
  7.5 0.6 constant_dynamic-slice_fusion.4
  8.1 0.0 all-gather.8.cloned.1.call-start
  8.2 0.7 all-gather.8.cloned.1.call-update
  9.0 0.7 constant_dynamic-slice_fusion.3
  9.7 34.2 %all_gather.27 = bf16[4096,4]{0,1:T(4,128)(2,1)S(1)} all-gather(bf16[128,4]{0,1:T(4,128)(2,1)S(1)} %constant_dynamic-slice_fusion.3), channel_id=1, replica_groups=mesh['seq'=32,'hid'=16] {'seq'}, dimensions={0}, use_global_device_ids=true | all-gather | bytes 33792 | tf_op jit(solution)/shard_map/all_gather | solution.py:86
  43.8 0.7 exponential_negate_fusion
  44.5 3.5 compare_select_fusion
  48.0 0.1 multiply_bitcast_fusion
  48.1 2.4 reduce-window.6
  50.5 0.1 slice.96
  50.6 0.1 copy.79
  50.7 0.1 copy.80
  50.8 0.1 broadcast_add_fusion
  50.9 0.9 constant_dynamic-slice_fusion.2
  51.8 0.2 slice_reduce_fusion
  52.1 0.1 bitcast_exponential_fusion
  52.1 32.9 %all-gather.10.cloned.1.call-done = bf16[4096,256]{1,0:T(8,128)(2,1)} async-done(((bf16[128,256]{1,0:T(8,128)(2,1)}), bf16[4096,256]{1,0:T(8,128)(2,1)}) %all-gather.10.cloned.1.call-update) | async-done | bytes 2097168 | tf_op jit(solution)/shard_map/all_gather | solution.py:85
  85.0 4.1 fusion.4
  89.2 2.1 collective-permute-start.1
  91.3 64.3 %all-gather.8.cloned.1.call-done = bf16[4096,256]{1,0:T(8,128)(2,1)} async-done(((bf16[128,256]{1,0:T(8,128)(2,1)}), bf16[4096,256]{1,0:T(8,128)(2,1)}) %all-gather.8.cloned.1.call-update) | async-done | bytes 2097168 | tf_op jit(solution)/shard_map/all_gather | solution.py:83
  155.6 4.1 convolution_convert_fusion.3
  159.8 2.1 collective-permute-start
  161.9 0.3 multiply_convert_fusion.5
  162.3 2.3 collective-permute-done
  164.7 0.3 multiply_convert_fusion.6
  165.0 0.2 reshape.122
  165.3 0.3 copy.81
  165.5 0.8 fusion.12
  166.3 0.3 while.26
  166.4 0.1 bitcast_add_fusion.2
  166.6 0.1 bitcast_add_fusion.2
  166.7 0.7 copy.84
  167.4 0.0 all-gather.12.cloned.1.call-start
  167.5 0.5 all-gather.12.cloned.1.call-update
  168.0 0.5 all-gather.14.cloned.1.call-update
  168.6 0.0 reduce-scatter.2.cloned.1.call-start
  168.7 1.3 dynamic-slice
  170.6 0.2 dynamic-update-slice
  170.9 44.1 %all-reduce = bf16[128]{0:T(256)(128)(2,1)S(1)} all-reduce(bf16[128]{0:T(256)(128)(2,1)S(1)} %dynamic-update-slice), channel_id=2, replica_groups=mesh['seq'=32,'hid'=16] {'seq'}, use_global_device_ids=true, to_apply=%add | all-reduce | flops 128 | bytes 512
  214.9 0.1 reshape.112
  215.1 0.1 broadcast_in_dim.25
  215.1 0.1 mul.255
  215.3 0.2 fusion.24
  215.5 21.5 %all-gather.16.cloned.1.call-done = bf16[128,128,64]{1,2,0:T(8,128)(2,1)} async-done(((bf16[4,128,64]{1,2,0:T(8,128)(2,1)}), bf16[128,128,64]{1,2,0:T(8,128)(2,1)}) %all-gather.16.cloned.1.call-update) | async-done | bytes 2097168 | tf_op jit(solution)/shard_map/all_gather | solution.py:24
  237.1 2.3 while.25
  237.1 0.9 constant_dynamic-slice_fusion.6
  237.9 0.1 copy.99
  238.1 0.1 convert_add_fusion.2
  238.2 0.9 constant_dynamic-slice_fusion.6
  239.1 0.1 copy.99
  239.2 0.1 convert_add_fusion.2
  239.4 0.1 multiply_add_fusion
  239.5 0.2 copy.86
  239.7 0.4 fusion.25
  240.1 0.8 fusion.2
  240.8 0.4 copy.93
  241.2 0.6 reshape.121
  241.8 65.7 %all-gather.12.cloned.1.call-done = bf16[4096,256]{1,0:T(8,128)(2,1)} async-done(((bf16[128,256]{1,0:T(8,128)(2,1)}), bf16[4096,256]{1,0:T(8,128)(2,1)}) %all-gather.12.cloned.1.call-update) | async-done | bytes 2097168 | tf_op jit(solution)/shard_map/all_gather | solution.py:84
  307.5 4.3 multiply_reduce_fusion
  311.8 40.3 %psum.7 = f32[512]{0:T(512)S(1)} all-reduce(f32[512]{0:T(512)S(1)} %get-tuple-element.172), channel_id=1, replica_groups=mesh['seq'=32,'hid'=16] {'hid'}, use_global_device_ids=true, to_apply=%region_9.10 | all-reduce | flops 512 | bytes 4096 | tf_op jit(solution)/shard_map/psum | solution.py:137
  352.1 25.9 %all-gather.14.cloned.1.call-done = bf16[4096,256]{1,0:T(8,128)(2,1)} async-done(((bf16[128,256]{1,0:T(8,128)(2,1)}), bf16[4096,256]{1,0:T(8,128)(2,1)}) %all-gather.14.cloned.1.call-update) | async-done | bytes 2097168 | tf_op jit(solution)/shard_map/all_gather | solution.py:87
  378.0 4.8 %convolution_convert_fusion = bf16[512,4096]{1,0:T(8,128)(2,1)} fusion(bf16[4096,256]{1,0:T(8,128)(2,1)} %all-gather.14.cloned.1.call-done, f32[512,256]{1,0:T(8,128)S(1)} %get-tuple-element.173, f32[256]{0:T(256)S(1)} %copy-done.1, f32[512]{0:T(512)S(1)} %add_rsqrt_fusion), kind=kOutput, calls=%fused_computation.8 | convolution fusion | flops 1076232192 | bytes 6818816 | tf_op jit(solution)/shard_map/dot_general | solution.py:139
  382.9 91.1 %reduce-scatter.2.cloned.1.call-done = bf16[512,256]{1,0:T(8,128)(2,1)} async-done(((bf16[512,4096]{1,0:T(8,128)(2,1)}), bf16[512,256]{1,0:T(8,128)(2,1)}) %reduce-scatter.2.cloned.1.call-update) | async-done | bytes 262160 | tf_op jit(solution)/shard_map/reduce_scatter | solution.py:142
  (38 shorter events, 0.5 us)
Async XLA Ops:
  6.5 1.0 copy-start
  6.5 78.5 %all-gather.10.cloned.1.call-start = ((), (), s32[]{:S(2)}) async-start(), calls=%async_computation.2 | async-start | bytes 2162688 | tf_op jit(solution)/shard_map/all_gather | solution.py:85
  8.1 147.5 %all-gather.8.cloned.1.call-start = ((), (), s32[]{:S(2)}) async-start(), calls=%async_computation.1 | async-start | bytes 2162688 | tf_op jit(solution)/shard_map/all_gather | solution.py:83
  8.9 228.1 %all-gather.16.cloned.1.call-start = ((), (), s32[]{:S(2)}) async-start(), calls=%async_computation.6 | async-start | bytes 2162688 | tf_op jit(solution)/shard_map/all_gather | solution.py:24
  44.5 7.5 %copy-start.2 = (f32[4,256]{1,0:T(4,128)S(1)}, f32[4,256]{1,0:T(4,128)}, u32[]{:S(2)}) copy-start(f32[4,256]{1,0:T(4,128)} %param.22) | copy-start | bytes 12292
  89.2 72.7 %collective-permute-start.1 = (bf16[3,256]{1,0:T(4,128)(2,1)S(1)}, bf16[3,256]{1,0:T(4,128)(2,1)S(1)}, u32[]{:S(2)}, u32[]{:S(2)}) collective-permute-start(bf16[3,256]{1,0:T(4,128)(2,1)S(1)} %slice.89), channel_id=1, source_target_pairs={{0,16},{16,32},{32,48},{48,64},{64,80},{80,96},{96,112},{112,128},... | collective-permute-start | bytes 4616 | tf_op jit(solution)/shard_map/ppermute | solution.py:18
  159.8 4.9 %collective-permute-start = (bf16[3,256]{1,0:T(4,128)(2,1)S(1)}, bf16[3,256]{1,0:T(4,128)(2,1)S(1)}, u32[]{:S(2)}, u32[]{:S(2)}) collective-permute-start(bf16[3,256]{1,0:T(4,128)(2,1)S(1)} %slice.84), channel_id=1, source_target_pairs={{0,16},{16,32},{32,48},{48,64},{64,80},{80,96},{96,112},{112,128},... | collective-permute-start | bytes 4616 | tf_op jit(solution)/shard_map/ppermute | solution.py:18
  166.3 48.7 %copy-start.3 = (f32[4]{0:T(128)S(1)}, f32[4]{0:T(128)}, u32[]{:S(2)}) copy-start(f32[4]{0:T(128)} %param.26) | copy-start | bytes 52
  167.4 140.1 %all-gather.12.cloned.1.call-start = ((), (), s32[]{:S(2)}) async-start(), calls=%async_computation.3 | async-start | bytes 2162688 | tf_op jit(solution)/shard_map/all_gather | solution.py:84
  168.0 210.0 %all-gather.14.cloned.1.call-start = ((), (), s32[]{:S(2)}) async-start(), calls=%async_computation.4 | async-start | bytes 2162688 | tf_op jit(solution)/shard_map/all_gather | solution.py:87
  168.6 305.3 %reduce-scatter.2.cloned.1.call-start = ((), (), s32[]{:S(2)}) async-start(), calls=%async_computation.5 | async-start | bytes 4456448 | tf_op jit(solution)/shard_map/reduce_scatter | solution.py:142
  241.8 136.2 %copy-start.1 = (f32[256]{0:T(256)S(1)}, f32[256]{0:T(256)}, u32[]{:S(2)}) copy-start(f32[256]{0:T(256)} %param.27) | copy-start | bytes 3076
Sparse Core Ops, SparseCore 0:
  9.5 75.5 all-gather.9
  87.1 68.4 all-gather.7
  167.5 69.4 all-gather.15
  239.0 68.4 all-gather.11
  309.5 68.4 all-gather.13
  383.0 90.8 reduce-scatter.1
where the time goes:
time: 483 us; the launch traced here: 481 us
  waiting for transfers between devices  306 us (63%)
  blocking collectives  119 us (25%)
  matrix products  22.9 us (5%)
  between operations  14.4 us (3%)
  local copies, waits for them, and re-layouts  9.82 us (2%)
  other arithmetic  4.96 us (1%)
    reduce_scatter x1, waiting for transfers between devices, local(): lax.psum_scatter(terms.astype(jnp.bfloat16), 'hid', scatter_dimension=1,...  91.1 us
    all_gather x1, waiting for transfers between devices, local(): piece_gate = lax.all_gather(w_gate, 'seq', axis=0, tiled=True)  65.7 us
    all_gather x1, waiting for transfers between devices, local(): piece_inner = lax.all_gather(w_inner, 'seq', axis=0, tiled=True)  64.3 us
    unnamed x1, blocking collectives  44.1 us
    psum x1, blocking collectives, local(): squares = lax.psum(jnp.sum(gated * gated, axis=1), 'hid')  40.3 us
    all_gather x1, blocking collectives, local(): piece_step = lax.all_gather(step_cols, 'seq', axis=0, tiled=True)  34.2 us
    all_gather x1, waiting for transfers between devices, local(): piece_groups = lax.all_gather(own_cols, 'seq', axis=0, tiled=True)  32.9 us
    all_gather x1, waiting for transfers between devices, local(): piece_out = lax.all_gather(w_out, 'seq', axis=0, tiled=True)  25.9 us
  transfers between devices with their start and end apart: 8, of which 7 were waited for; matrix products, arithmetic and copies ran while one was open for 6% of the time, Pallas kernels for 0%

commit v1 on v0

--- a/solution.py
+++ b/solution.py
@@ -83,8 +83,11 @@
     piece_inner = lax.all_gather(w_inner, "seq", axis=0, tiled=True)
     piece_gate = lax.all_gather(w_gate, "seq", axis=0, tiled=True)
     piece_groups = lax.all_gather(own_cols, "seq", axis=0, tiled=True)
-    piece_step = lax.all_gather(step_cols, "seq", axis=0, tiled=True)
-    piece_out = lax.all_gather(w_out, "seq", axis=0, tiled=True)
+    piece_step, piece_out = jnp.split(
+        lax.all_gather(jnp.concatenate([step_cols, w_out], axis=1), "seq", axis=0, tiled=True),
+        [step_cols.shape[1]],
+        axis=1,
+    )
     acc_inner = jnp.dot(activations, piece_inner, preferred_element_type=jnp.float32)
     acc_gate = jnp.dot(activations, piece_gate, preferred_element_type=jnp.float32)
     acc_groups = jnp.dot(activations, piece_groups, preferred_element_type=jnp.float32)

time: 483 us -> 520 us (1.077)
  waiting for transfers between devices: 306 us -> 371 us
  blocking collectives: 119 us -> 86.6 us
    all_gather x1, waiting for transfers between devices: 32.9 us -> 71.1 us  [local(): piece_groups = lax.all_gather(own_cols, 'seq', axis=0, tiled=True)]
    all_gather x1, waiting for transfers between devices: 25.9 us -> 61.9 us  [local(): lax.all_gather(jnp.concatenate([step_cols, w_out], axis=1), 'seq', axis=0...]
    all_gather x1 -> x0, blocking collectives: 34.2 us -> none  [local(): piece_step = lax.all_gather(step_cols, 'seq', axis=0, tiled=True)]
  transfers between devices with their start and end apart: 8 -> 8, of which waited for: 7 -> 7; matrix products, arithmetic and copies ran while one was open for 6% -> 4% of each run, Pallas kernels for 0% -> 0%
where the time goes in v1:
time: 520 us; the launch traced here: 518 us
  waiting for transfers between devices  371 us (71%)
  blocking collectives  86.6 us (17%)
  matrix products  23.5 us (5%)
  between operations  14.4 us (3%)
  local copies, waits for them, and re-layouts  11.6 us (2%)
  other arithmetic  6.53 us (1%)
    reduce_scatter x1, waiting for transfers between devices, local(): lax.psum_scatter(terms.astype(jnp.bfloat16), 'hid', scatter_dimension=1,...  86.2 us
    all_gather x1, waiting for transfers between devices, local(): piece_groups = lax.all_gather(own_cols, 'seq', axis=0, tiled=True)  71.1 us
    all_gather x1, waiting for transfers between devices, local(): piece_gate = lax.all_gather(w_gate, 'seq', axis=0, tiled=True)  64.9 us
    all_gather x1, waiting for transfers between devices, local(): piece_inner = lax.all_gather(w_inner, 'seq', axis=0, tiled=True)  64.3 us
    all_gather x1, waiting for transfers between devices, local(): lax.all_gather(jnp.concatenate([step_cols, w_out], axis=1), 'seq', axis=0...  61.9 us
    unnamed x1, blocking collectives  46.3 us
    psum x1, blocking collectives, local(): squares = lax.psum(jnp.sum(gated * gated, axis=1), 'hid')  40.3 us
    all_gather x1, waiting for transfers between devices, carried_in(): lax.all_gather(a.astype(kind), axis)  18.8 us
  transfers between devices with their start and end apart: 8, of which 7 were waited for; matrix products, arithmetic and copies ran while one was open for 4% of the time, Pallas kernels for 0%

profile of v1, /device:TPU:32, one launch (start us, length us, event | category | flops | bytes accessed | tf_op | source)
XLA Modules:
  0.0 518.3 jit_solution(15758145077638880156)
XLA Ops:
  6.5 0.9 copy-done
  7.5 0.6 constant_dynamic-slice_fusion.4
  8.1 0.0 all-gather.8.cloned.1.call-start
  8.2 0.7 all-gather.8.cloned.1.call-update
  8.9 0.7 constant_dynamic-slice_fusion.3
  9.6 0.1 copy.103
  9.8 1.6 pad_maximum_fusion.2
  11.4 0.0 all-gather.16.cloned.1.call-start
  11.4 0.9 constant_dynamic-slice_fusion.2
  12.4 0.7 exponential_negate_fusion
  13.0 0.8 fusion.27
  13.9 71.1 %all-gather.10.cloned.1.call-done = bf16[4096,256]{1,0:T(8,128)(2,1)} async-done(((bf16[128,256]{1,0:T(8,128)(2,1)}), bf16[4096,256]{1,0:T(8,128)(2,1)}) %all-gather.10.cloned.1.call-update) | async-done | bytes 2097168 | tf_op jit(solution)/shard_map/all_gather | solution.py:85
  85.0 4.1 fusion.5
  89.2 2.1 collective-permute-start.1
  91.3 64.3 %all-gather.8.cloned.1.call-done = bf16[4096,256]{1,0:T(8,128)(2,1)} async-done(((bf16[128,256]{1,0:T(8,128)(2,1)}), bf16[4096,256]{1,0:T(8,128)(2,1)}) %all-gather.8.cloned.1.call-update) | async-done | bytes 2097168 | tf_op jit(solution)/shard_map/all_gather | solution.py:83
  155.6 4.1 convolution_convert_fusion.3
  159.8 2.1 collective-permute-start
  161.9 0.3 multiply_convert_fusion.5
  162.3 2.3 collective-permute-done
  164.7 0.3 multiply_convert_fusion.6
  165.0 0.2 reshape.122
  165.3 0.3 copy.86
  165.5 61.9 %all-gather.12.cloned.1.call-done = bf16[4096,260]{1,0:T(8,128)(2,1)} async-done(((bf16[128,260]{1,0:T(8,128)(2,1)}), bf16[4096,260]{1,0:T(8,128)(2,1)}) %all-gather.12.cloned.1.call-update) | async-done | bytes 2129936 | tf_op jit(solution)/shard_map/all_gather | solution.py:87
  227.4 3.7 compare_select_fusion
  231.2 0.1 multiply_bitcast_fusion
  231.3 2.4 reduce-window.6
  233.7 0.1 slice.96
  233.8 0.1 copy.84
  233.9 0.1 copy.85
  234.0 0.1 broadcast_add_fusion
  234.1 0.2 slice_reduce_fusion
  234.3 0.1 bitcast_exponential_fusion
  234.4 0.8 fusion.14
  235.3 0.3 while.26
  235.3 0.1 bitcast_add_fusion.2
  235.5 0.1 bitcast_add_fusion.2
  235.6 0.7 copy.89
  236.4 0.5 all-gather.14.cloned.1.call-update
  237.0 0.1 broadcast_in_dim.25
  237.1 0.1 mul.255
  237.1 1.3 dynamic-slice
  239.2 0.2 fusion.28
  239.5 0.2 dynamic-update-slice
  239.7 46.3 %all-reduce = bf16[128]{0:T(256)(128)(2,1)S(1)} all-reduce(bf16[128]{0:T(256)(128)(2,1)S(1)} %dynamic-update-slice), channel_id=2, replica_groups=mesh['seq'=32,'hid'=16] {'seq'}, use_global_device_ids=true, to_apply=%add | all-reduce | flops 128 | bytes 512
  286.0 0.1 reshape.112
  286.1 18.8 %all-gather.16.cloned.1.call-done = bf16[128,128,64]{1,2,0:T(8,128)(2,1)} async-done(((bf16[4,128,64]{1,2,0:T(8,128)(2,1)}), bf16[128,128,64]{1,2,0:T(8,128)(2,1)}) %all-gather.16.cloned.1.call-update) | async-done | bytes 2097168 | tf_op jit(solution)/shard_map/all_gather | solution.py:24
  305.0 2.3 while.25
  305.0 0.9 constant_dynamic-slice_fusion.6
  305.9 0.1 copy.105
  306.0 0.1 convert_add_fusion.2
  306.2 0.9 constant_dynamic-slice_fusion.6
  307.0 0.1 copy.105
  307.2 0.1 convert_add_fusion.2
  307.3 0.1 multiply_add_fusion
  307.4 0.2 copy.91
  307.6 0.4 fusion.29
  308.0 0.7 fusion.3
  308.7 0.4 copy.98
  309.1 1.4 reshape.121
  310.6 64.9 %all-gather.14.cloned.1.call-done = bf16[4096,256]{1,0:T(8,128)(2,1)} async-done(((bf16[128,256]{1,0:T(8,128)(2,1)}), bf16[4096,256]{1,0:T(8,128)(2,1)}) %all-gather.14.cloned.1.call-update) | async-done | bytes 2097168 | tf_op jit(solution)/shard_map/all_gather | solution.py:84
  375.4 5.1 multiply_reduce_fusion
  380.5 40.3 %psum.7 = f32[512]{0:T(512)S(1)} all-reduce(f32[512]{0:T(512)S(1)} %get-tuple-element.172), channel_id=1, replica_groups=mesh['seq'=32,'hid'=16] {'hid'}, use_global_device_ids=true, to_apply=%region_9.10 | all-reduce | flops 512 | bytes 4096 | tf_op jit(solution)/shard_map/psum | solution.py:140
  420.8 4.4 convolution_convert_fusion
  425.2 86.2 %reduce-scatter.2.cloned.1.call-done = bf16[512,256]{1,0:T(8,128)(2,1)} async-done(((bf16[512,4096]{1,0:T(8,128)(2,1)}), bf16[512,256]{1,0:T(8,128)(2,1)}) %reduce-scatter.2.cloned.1.call-update) | async-done | bytes 262160 | tf_op jit(solution)/shard_map/reduce_scatter | solution.py:145
  (43 shorter events, 0.6 us)
Async XLA Ops:
  6.5 1.0 copy-start
  6.5 78.5 %all-gather.10.cloned.1.call-start = ((), (), s32[]{:S(2)}) async-start(), calls=%async_computation.2 | async-start | bytes 2162688 | tf_op jit(solution)/shard_map/all_gather | solution.py:85
  8.1 147.5 %all-gather.8.cloned.1.call-start = ((), (), s32[]{:S(2)}) async-start(), calls=%async_computation.1 | async-start | bytes 2162688 | tf_op jit(solution)/shard_map/all_gather | solution.py:83
  8.9 218.5 %all-gather.12.cloned.1.call-start = ((), (), s32[]{:S(2)}) async-start(), calls=%async_computation.3 | async-start | bytes 3244032 | tf_op jit(solution)/shard_map/all_gather | solution.py:87
  11.4 293.6 %all-gather.16.cloned.1.call-start = ((), (), s32[]{:S(2)}) async-start(), calls=%async_computation.6 | async-start | bytes 2162688 | tf_op jit(solution)/shard_map/all_gather | solution.py:24
  89.2 72.8 %collective-permute-start.1 = (bf16[3,256]{1,0:T(4,128)(2,1)S(1)}, bf16[3,256]{1,0:T(4,128)(2,1)S(1)}, u32[]{:S(2)}, u32[]{:S(2)}) collective-permute-start(bf16[3,256]{1,0:T(4,128)(2,1)S(1)} %slice.89), channel_id=1, source_target_pairs={{0,16},{16,32},{32,48},{48,64},{64,80},{80,96},{96,112},{112,128},... | collective-permute-start | bytes 4616 | tf_op jit(solution)/shard_map/ppermute | solution.py:18
  159.7 67.7 %copy-start.5 = (f32[4]{0:T(128)S(1)}, f32[4]{0:T(128)}, u32[]{:S(2)}) copy-start(f32[4]{0:T(128)} %param.24) | copy-start | bytes 52
  159.8 4.9 collective-permute-start
  165.0 66.2 %copy-start.2 = (bf16[512,256]{1,0:T(8,128)(2,1)}, bf16[512,256]{1,0:T(8,128)(2,1)S(1)}, u32[]{:S(2)}) copy-start(bf16[512,256]{1,0:T(8,128)(2,1)S(1)} %multiply_convert_fusion.6) | copy-start | bytes 786436
  235.2 1.7 copy-start.4
  236.3 139.1 %all-gather.14.cloned.1.call-start = ((), (), s32[]{:S(2)}) async-start(), calls=%async_computation.4 | async-start | bytes 2162688 | tf_op jit(solution)/shard_map/all_gather | solution.py:84
  236.9 274.5 %reduce-scatter.2.cloned.1.call-start = ((), (), s32[]{:S(2)}) async-start(), calls=%async_computation.5 | async-start | bytes 4456448 | tf_op jit(solution)/shard_map/reduce_scatter | solution.py:145
  310.6 110.3 %copy-start.1 = (bf16[4096,260]{1,0:T(8,128)(2,1)S(1)}, bf16[4096,260]{1,0:T(8,128)(2,1)}, u32[]{:S(2)}) copy-start(bf16[4096,260]{1,0:T(8,128)(2,1)} %all-gather.12.cloned.1.call-done) | copy-start | bytes 6389764
  310.6 110.3 %copy-start.3 = (f32[256]{0:T(256)S(1)}, f32[256]{0:T(256)}, u32[]{:S(2)}) copy-start(f32[256]{0:T(256)} %param.27) | copy-start | bytes 3076
Sparse Core Ops, SparseCore 0:
  9.5 75.5 all-gather.9
  87.1 68.4 all-gather.7
  157.7 69.6 all-gather.11
  236.4 68.4 all-gather.15
  306.9 68.4 all-gather.13
  425.3 86.0 reduce-scatter.1
